TPU v7x, 32 devices: a whole 2x2x4 slice. The times are simulated.
32 devices in a mesh: grp: 2 (over y), ctx: 4 (over z), kvh: 2 (over x), sub: 2 (over core).
Axes of the slice: x: 2, y: 2, z: 4, core: 2. Of those that a mesh axis runs over, the one named last changes fastest.
Arguments:
- queries: bfloat16 [1024, 8, 8, 128], P(('grp', 'ctx'), 'kvh', 'sub'), parts along dimension 0
- new_keys: bfloat16 [1024, 8, 128], P(('grp', 'ctx'), 'kvh'), parts along dimension 0
- new_values: bfloat16 [1024, 8, 128], P(('grp', 'ctx'), 'kvh'), parts along dimension 0, may hold values from -6 to 6
- cache_keys: bfloat16 [16384, 8, 128], P(('grp', 'ctx'), 'kvh'), parts along dimension 0, may hold values from -16 to 16
- cache_values: bfloat16 [16384, 8, 128], P(('grp', 'ctx'), 'kvh'), parts along dimension 0, may hold values from -6 to 6
- vertical_pool: int32 [16], P(('grp', 'ctx')), parts along dimension 0, may hold values from 0 to 15, as said below
- vertical_lists: int32 [8, 6], P(('grp', 'ctx')), parts along dimension 0, may hold values from 0 to 7, as said below
- slash_lists: int32 [8, 2], P(('grp', 'ctx')), parts along dimension 0, may hold values from 0 to 1, as said below
- list_counts: int32 [8, 2], P(('grp', 'ctx')), parts along dimension 0, may hold values from 1 to 6, as said below
Outputs:
- attention: bfloat16 [1024, 8, 8, 128], P(('grp', 'ctx'), 'kvh', 'sub'), parts along dimension 0
There are 2 independent parts, one for each index of `grp`. A program takes and returns all parts, laid end to end along the dimension named above; each array names one. Nothing has to cross between parts.
Inputs may be any that keep to these rules, and one draw needn't show every extreme that they name: `vertical_pool`: the 2 entries of one index of ctx are distinct. `vertical_lists`: in row b the first list_counts[b, 0] entries are distinct; later entries are never read. `slash_lists`: row b begins with 0; its first list_counts[b, 1] entries are distinct and none exceeds b or 1 plus b modulo 1; later entries are never read. `list_counts`: column 0 lies between 1 and 6, column 1 between 1 and 2, each reached in every draw.
All inputs are finite; a program needn't handle non-finite values.
Results may differ from a plain program's by a relative error of at most 0.014.
Values may be sent and summed in bfloat16 or wider, within the bound.
A program may use at most 64 MiB of HBM per device.

v0:
```python
import jax
import jax.numpy as jnp
from jax import lax
from jax.sharding import PartitionSpec as P

BLK = 128


group_width = 8


def from_behind(block, axis, distance):
    devices = range(lax.axis_size(axis))
    route = [(i - distance, i) for i in devices if i - distance in devices]
    return lax.ppermute(block, axis, route)


def block_update(carry_state, query_block, block_keys, block_values, visible):
    row_peak, row_total, numerator = carry_state
    score_scale = query_block.shape[-1] ** (-0.5)
    scores = (
        jnp.einsum("rkgd,ckd->rkgc", query_block, block_keys, preferred_element_type=jnp.float32)
        * score_scale
    )
    scores = jnp.where(visible, scores, -jnp.inf)
    new_peak = jnp.maximum(row_peak, jnp.max(scores, axis=3))
    factor = jnp.exp(row_peak - new_peak)
    weights = jnp.exp(scores - new_peak[..., None])
    row_total = row_total * factor + jnp.sum(weights, axis=3)
    numerator = numerator * factor[..., None] + jnp.einsum(
        "rkgc,ckd->rkgd",
        weights.astype(jnp.bfloat16),
        block_values,
        preferred_element_type=jnp.float32,
    )
    return (new_peak, row_total, numerator)


def blank_state(query_block):
    rows_shape = query_block.shape[:3]
    return (
        jnp.full(rows_shape, -jnp.inf, jnp.float32),
        jnp.zeros(rows_shape, jnp.float32),
        jnp.zeros(query_block.shape, jnp.float32),
    )


def vertical_range(
    carry_state, query_block, pool_keys, pool_values, entries, start_entry, stop_entry
):
    list_length = entries.shape[0]
    padded_length = -(-list_length // group_width) * group_width
    padded_entries = jnp.pad(entries, (0, padded_length - list_length))
    block_size = pool_keys.shape[1]
    kv_width = pool_keys.shape[2]
    head_dim = pool_keys.shape[3]
    first_group = start_entry // group_width
    last_group = jnp.where(
        stop_entry > start_entry, (stop_entry + group_width - 1) // group_width, first_group
    )

    def group_step(group_index, inner_state):
        base = group_index * group_width
        slots = lax.dynamic_slice_in_dim(padded_entries, base, group_width)
        places = base + jnp.arange(group_width, dtype=jnp.int32)
        live = (places >= start_entry) & (places < stop_entry)
        slots = jnp.where(live, slots, 0)
        group_keys = jnp.take(pool_keys, slots, axis=0).reshape(
            group_width * block_size, kv_width, head_dim
        )
        group_values = jnp.take(pool_values, slots, axis=0).reshape(
            group_width * block_size, kv_width, head_dim
        )
        visible = jnp.repeat(live, block_size)[None, None, None, :]
        return block_update(inner_state, query_block, group_keys, group_values, visible)

    return lax.fori_loop(first_group, last_group, group_step, carry_state)


def slash_range(
    carry_state, query_block, window_keys, window_values, entries, entry_count, window_base
):
    block_size = query_block.shape[0]
    row_ids = lax.broadcasted_iota(jnp.int32, (block_size, 1, 1, block_size), 0)
    col_ids = lax.broadcasted_iota(jnp.int32, (block_size, 1, 1, block_size), 3)
    causal = col_ids <= row_ids

    def slash_step(step_index, inner_state):
        offset = entries[step_index]
        target = window_base - offset
        return block_update(
            inner_state,
            query_block,
            window_keys[target],
            window_values[target],
            causal | (offset > 0),
        )

    return lax.fori_loop(0, entry_count, slash_step, carry_state)


def shards(
    queries,
    new_keys,
    new_values,
    cache_keys,
    cache_values,
    vertical_pool,
    vertical_lists,
    slash_lists,
    list_counts,
):
    queries = lax.all_to_all(queries, "sub", split_axis=1, concat_axis=2, tiled=True)
    kv_width = queries.shape[1]
    first_head = lax.axis_index("sub") * kv_width
    new_keys = lax.dynamic_slice_in_dim(new_keys, first_head, kv_width, 1)
    new_values = lax.dynamic_slice_in_dim(new_values, first_head, kv_width, 1)
    cache_keys = lax.dynamic_slice_in_dim(cache_keys, first_head, kv_width, 1)
    cache_values = lax.dynamic_slice_in_dim(cache_values, first_head, kv_width, 1)
    tokens, kv_width, groups, head_dim = queries.shape
    block_size = BLK
    query_count = tokens // block_size
    cache_count = cache_keys.shape[0] // block_size
    chosen_keys = jnp.take(
        cache_keys.reshape(cache_count, block_size, kv_width, head_dim), vertical_pool, axis=0
    )
    chosen_values = jnp.take(
        cache_values.reshape(cache_count, block_size, kv_width, head_dim), vertical_pool, axis=0
    )
    pool_keys, pool_values = (
        lax.all_gather(chosen_keys, "ctx", axis=0, tiled=True),
        lax.all_gather(chosen_values, "ctx", axis=0, tiled=True),
    )
    earlier_keys, earlier_values = from_behind((new_keys, new_values), "ctx", 1)
    window_keys = jnp.concatenate([earlier_keys, new_keys], 0).reshape(
        2 * query_count, block_size, kv_width, head_dim
    )
    window_values = jnp.concatenate([earlier_values, new_values], 0).reshape(
        2 * query_count, block_size, kv_width, head_dim
    )
    query_grid = queries.reshape(query_count, block_size, kv_width, groups, head_dim)
    query_block = query_grid[0]
    carry_state = vertical_range(
        blank_state(query_block),
        query_block,
        pool_keys,
        pool_values,
        vertical_lists[0],
        0,
        list_counts[0, 0],
    )
    carry_state = slash_range(
        carry_state,
        query_block,
        window_keys,
        window_values,
        slash_lists[0],
        list_counts[0, 1],
        query_count,
    )
    results = [(carry_state[2] / carry_state[1][..., None]).astype(jnp.bfloat16)]
    attention = jnp.stack(results).reshape(tokens, kv_width, groups, head_dim)
    attention = lax.all_to_all(attention, "sub", split_axis=2, concat_axis=1, tiled=True)
    return attention


def solution(mesh):
    in_specs = (
        P(("grp", "ctx"), "kvh", "sub", None),
        P(("grp", "ctx"), "kvh", None),
        P(("grp", "ctx"), "kvh", None),
        P(("grp", "ctx"), "kvh", None),
        P(("grp", "ctx"), "kvh", None),
        P(("grp", "ctx")),
        P(("grp", "ctx"), None),
        P(("grp", "ctx"), None),
        P(("grp", "ctx"), None),
    )
    out_specs = P(("grp", "ctx"), "kvh", "sub", None)
    return jax.shard_map(shards, mesh=mesh, in_specs=in_specs, out_specs=out_specs, check_vma=False)
```

profile of v0, /device:TPU:11, one launch (start us, length us, event | category | flops | bytes accessed | tf_op | source)
XLA Modules:
  0.0 81.0 jit_solution(13073453692627988629)
XLA Ops:
  0.0 2.0 %copy.62 = bf16[128,4,4,128]{3,2,0,1:T(4,128)(2,1)} copy(bf16[128,4,4,128]{3,2,1,0:T(4,128)(2,1)} %param.17) | data formatting | bytes 1048576 | tf_op args[0]
  2.1 4.2 %all-to-all-start = ((bf16[128,4,4,128]{3,2,0,1:T(4,128)(2,1)}), bf16[128,4,4,128]{3,2,0,1:T(4,128)(2,1)S(1)}, u32[]{:S(2)}, u32[]{:S(2)}) async-start(bf16[128,4,4,128]{3,2,0,1:T(4,128)(2,1)} %copy.62), calls=%async_computation | async-start | bytes 1048576 | tf_op jit(solution)/shard_map/all_to_all | solution.py:113
  6.2 0.1 constant_dynamic-slice_fusion.1
  6.3 3.2 %collective-permute-start = (bf16[128,2,128]{2,0,1:T(8,128)(2,1)S(1)}, bf16[128,2,128]{2,0,1:T(8,128)(2,1)S(1)}, u32[]{:S(2)}, u32[]{:S(2)}) collective-permute-start(bf16[128,2,128]{2,0,1:T(8,128)(2,1)S(1)} %copy.87), channel_id=1, source_target_pairs={{0,4},{4,8},{8,12},{1,5},{5,9},{9,13},{2,6},{6,10},{10,14},{3,7},{... | collective-permute-start | bytes 196616 | tf_op jit(solution)/shard_map/ppermute | solution.py:15
  9.5 1.0 %constant_dynamic-slice_fusion = bf16[128,2,128]{2,1,0:T(2,128)(2,1)S(1)} fusion(bf16[128,4,128]{2,1,0:T(4,128)(2,1)} %param.19, s32[]{:T(128)S(6)} %select_n.63), kind=kLoop, calls=%fused_computation.58 | loop fusion | bytes 131076 | tf_op jit(solution)/shard_map/dynamic_slice | solution.py:117
  10.5 3.2 %collective-permute-start.1 = (bf16[128,2,128]{2,0,1:T(8,128)(2,1)S(1)}, bf16[128,2,128]{2,0,1:T(8,128)(2,1)}, u32[]{:S(2)}, u32[]{:S(2)}) collective-permute-start(bf16[128,2,128]{2,0,1:T(8,128)(2,1)S(1)} %copy.88), channel_id=1, source_target_pairs={{0,4},{4,8},{8,12},{1,5},{5,9},{9,13},{2,6},{6,10},{10,14},{3,7},{... | collective-permute-start | bytes 196616 | tf_op jit(solution)/shard_map/ppermute | solution.py:15
  13.7 1.3 %fusion.36 = (s32[1,1]{1,0:T(1,128)}, s32[1,1]{1,0:T(1,128)}) fusion(s32[1,2]{1,0:T(1,128)} %param.25), kind=kLoop, calls=%fused_computation.63 | loop fusion | bytes 16 | tf_op jit(solution)/shard_map/slice | solution.py:158
  16.2 0.7 compare_select_fusion.1
  16.9 0.7 compare_and_fusion.2
  17.5 3.8 %constant_dynamic-slice_fusion.2 = (bf16[2048,2,128]{2,1,0:T(2,128)(2,1)S(1)}, bf16[2048,2,128]{2,1,0:T(2,128)(2,1)S(1)}) fusion(bf16[2048,4,128]{2,1,0:T(4,128)(2,1)} %param.21, s32[]{:T(128)S(6)} %select_n.63, bf16[2048,4,128]{2,1,0:T(4,128)(2,1)} %param.20), kind=kLoop, calls=%fused_computation.60 | loop fusion | bytes 4194308 | tf_op jit(solution)/shard_map/dynamic_slice | solution.py:119
  21.3 0.1 copy.89
  21.4 0.1 copy.61
  21.6 0.1 copy.90
  21.7 0.1 copy.65
  21.8 0.6 gather_fusion.2
  22.4 0.6 gather_fusion.3
  23.0 0.1 broadcast_select_fusion.2
  23.1 11.9 %all_gather.6 = bf16[8,128,2,128]{3,1,2,0:T(8,128)(2,1)S(1)} all-gather(bf16[2,128,2,128]{3,1,2,0:T(8,128)(2,1)S(1)} %get-tuple-element.337), channel_id=1, replica_groups=mesh['grp'=2,'ctx'=4,'kvh'=2,'sub'=2] {'ctx'}, dimensions={0}, use_global_device_ids=true | all-gather | bytes 655360 | tf_op jit(solution)/shard_map/all_gather | solution.py:131
  35.0 0.5 copy.66
  35.5 11.8 %all_gather.7 = bf16[8,128,2,128]{3,1,2,0:T(8,128)(2,1)S(1)} all-gather(bf16[2,128,2,128]{3,1,2,0:T(8,128)(2,1)S(1)} %get-tuple-element.336), channel_id=1, replica_groups=mesh['grp'=2,'ctx'=4,'kvh'=2,'sub'=2] {'ctx'}, dimensions={0}, use_global_device_ids=true | all-gather | bytes 655360 | tf_op jit(solution)/shard_map/all_gather | solution.py:132
  47.3 0.5 copy.67
  47.8 0.1 copy.63
  48.0 0.1 broadcast_in_dim.72
  48.1 0.0 copy-start.4
  48.1 10.8 %while.31 = (s32[]{:T(128)}, f32[128,2,8]{0,2,1:T(8,128)S(1)}, f32[128,2,8]{0,2,1:T(8,128)S(1)}, f32[128,2,8,128]{0,3,2,1:T(8,128)S(1)}, s32[]{:T(128)}, /*index...) while((s32[]{:T(128)}, f32[128,2,8]{0,2,1:T(8,128)S(1)}, ...), condition=%wide.region_3.6_spmd, body=%wide.region_0.5_spmd.sunk | while | flops 1097864192 | bytes 37364096 | solution.py:77
  48.3 0.0 copy-start.1
  48.3 0.6 compare_and_fusion.5
  48.9 1.6 %gather_fusion = bf16[8,128,2,128]{3,2,1,0:T(2,128)(2,1)S(1)} fusion(bf16[8,128,2,128]{3,2,1,0:T(2,128)(2,1)S(1)} %get-tuple-element.517, s32[1024]{0:T(1024)S(1)} %pad_clamp_fusion.3), kind=kCustom, calls=%fused_computation.3.clone.clone.1 | custom fusion | bytes 1048608 | tf_op jit(solution)/shard_map/while/body/jit(_take)/gather | solution.py:71
  50.5 1.6 %gather_fusion.1 = bf16[8,128,2,128]{3,2,1,0:T(2,128)(2,1)S(1)} fusion(bf16[8,128,2,128]{3,2,1,0:T(2,128)(2,1)S(1)} %get-tuple-element.515, s32[1024]{0:T(1024)S(1)} %pad_clamp_fusion.3), kind=kCustom, calls=%fused_computation.1.clone.clone.1 | custom fusion | bytes 1048608 | tf_op jit(solution)/shard_map/while/body/jit(_take)/gather | solution.py:68
  52.2 1.0 %broadcast_select_fusion.5 = (bf16[8,128,2,128]{3,2,1,0:T(2,128)(2,1)S(1)}, bf16[8,128,2,128]{3,2,1,0:T(2,128)(2,1)S(1)}) fusion(bf16[8,128,2,128]{3,2,1,0:T(2,128)(2,1)S(1)} %gather_fusion, pred[8]{0:T(512)(128)(4,1)S(1)} %get-tuple-element.464, bf16[8,128,2,128]{3,2,1,0:T(2,128)(2,1)S(1)} %gather_fusion.1), kind=kLoop, calls=%fused_computation.35.clone.1 | loop fusion | flops 524288 | bytes 2097160 | tf_op jit(solution)/shard_map/while/body/jit(_take)/select_n | solution.py:71
  53.1 0.1 broadcast_bitcast_fusion.2
  53.2 1.3 %bitcast_reduce_fusion.2 = (f32[128,2,8]{0,2,1:T(8,128)S(1)}, f32[2,1024,128,8]{2,1,3,0:T(8,128)S(1)}) fusion(pred[1024]{0:T(1024)(128)(4,1)S(1)} %broadcast_bitcast_fusion.2, bf16[128,2,8,128]{3,0,2,1:T(8,128)(2,1)S(1)} %get-tuple-element.516, bf16[1024,2,128,1]{2,1,0,3:T(2,128)(2,1)S(1)} %bitcast.107), kind=kOutput, calls=%fused_computation.26.clone.1 | convolution fusion | flops 543160320 | bytes 9446400 | tf_op jit(solution)/shard_map/while/body/rkgd,ckd->rkgc/dot_general | solution.py:22
  54.5 2.2 %fusion.54 = f32[128,2,8]{0,2,1:T(8,128)S(1)} fusion(f32[2,1024,128,8]{2,1,3,0:T(8,128)S(1)} %get-tuple-element.467, f32[128,2,8]{0,2,1:T(8,128)S(1)} %max.12, pred[1024]{0:T(1024)(128)(4,1)S(1)} %broadcast_bitcast_fusion.2), kind=kLoop, calls=%fused_computation.30.clone.1 | loop fusion | flops 8386560 | bytes 8406016 | tf_op jit(solution)/shard_map/while/body/reduce_sum | solution.py:29
  56.7 0.0 copy-start.2
  56.8 2.2 %fusion.55 = f32[128,2,8,128]{0,3,2,1:T(8,128)S(1)} fusion(f32[2,1024,128,8]{2,1,3,0:T(8,128)S(1)} %get-tuple-element.467, f32[128,2,8]{0,2,1:T(8,128)S(1)} %max.12, pred[1024]{0:T(1024)(128)(4,1)S(1)} %broadcast_bitcast_fusion.2, f32[128,2,8,128]{0,3,2,1:T(8,128)S(1)} %get-tuple-element.499, bf16[1024,2,128,1]{2,1,0,3:T(2,128)(2,1)S(1)} %bitcast.108, ...), kind=kOutput, calls=%fused_computation.34.clone.1 | convolution fusion | flops 545783808 | bytes 11027456 | tf_op jit(solution)/shard_map/while/body/rkgc,ckd->rkgd/dot_general | solution.py:30
  59.0 0.9 %pad_maximum_fusion.1 = bf16[256,2,128]{2,0,1:T(8,128)(2,1)S(1)} fusion(bf16[128,2,128]{2,0,1:T(8,128)(2,1)S(1)} %copy.88, bf16[128,2,128]{2,0,1:T(8,128)(2,1)} %collective-permute-done.1), kind=kLoop, calls=%fused_computation.52 | loop fusion | flops 262144 | bytes 262144 | tf_op jit(solution)/shard_map/concatenate | solution.py:138
  59.9 9.6 %while.32 = (s32[]{:T(128)}, f32[128,2,8]{0,2,1:T(8,128)S(1)}, f32[128,2,8]{0,2,1:T(8,128)S(1)}, f32[128,2,8,128]{0,3,2,1:T(8,128)S(1)}, s32[]{:T(128)}, /*index...) while((s32[]{:T(128)}, f32[128,2,8]{0,2,1:T(8,128)S(1)}, ...), condition=%wide.region_7.10_spmd.clone, body=%wide.region_4.9_spmd.clone.sunk | while | flops 136613888 | bytes 6062331 | solution.py:99
  60.5 0.7 dynamic_slice.57
  63.3 0.3 fusion.60
  63.6 0.2 fusion.61
  63.8 0.6 fusion.62
  65.0 0.7 dynamic_slice.57
  67.7 0.3 fusion.60
  68.1 0.2 fusion.61
  68.3 0.6 fusion.62
  69.5 0.1 fusion.34
  69.6 10.2 %all_to_all.36 = bf16[128,2,8,128]{0,3,1,2:T(8,128)(2,1)S(1)} all-to-all(bf16[128,2,8,128]{0,3,1,2:T(8,128)(2,1)S(1)} %fusion.34), channel_id=1, replica_groups=mesh['grp'=2,'ctx'=4,'kvh'=2,'sub'=2] {'sub'}, dimensions={2} | all-to-all | bytes 1048576 | tf_op jit(solution)/shard_map/all_to_all | solution.py:163
  79.8 1.2 %copy.74 = bf16[128,2,2,4,128]{4,3,2,1,0:T(4,128)(2,1)} copy(bf16[128,2,2,4,128]{0,4,2,3,1:T(8,128)(2,1)S(1)} %bitcast.112) | data formatting | bytes 1048576 | tf_op jit(solution)/shard_map/all_to_all | solution.py:163
  (30 shorter events, 0.2 us)
Async XLA Ops:
  0.0 6.2 %copy-start = (bf16[128,4,128]{2,1,0:T(4,128)(2,1)S(1)}, bf16[128,4,128]{2,1,0:T(4,128)(2,1)}, u32[]{:S(2)}) copy-start(bf16[128,4,128]{2,1,0:T(4,128)(2,1)} %param.18) | copy-start | bytes 393220
  2.1 45.8 %all-to-all-start = ((bf16[128,4,4,128]{3,2,0,1:T(4,128)(2,1)}), bf16[128,4,4,128]{3,2,0,1:T(4,128)(2,1)S(1)}, u32[]{:S(2)}, u32[]{:S(2)}) async-start(bf16[128,4,4,128]{3,2,0,1:T(4,128)(2,1)} %copy.62), calls=%async_computation | async-start | bytes 1048576 | tf_op jit(solution)/shard_map/all_to_all | solution.py:113
  6.3 52.7 %collective-permute-start = (bf16[128,2,128]{2,0,1:T(8,128)(2,1)S(1)}, bf16[128,2,128]{2,0,1:T(8,128)(2,1)S(1)}, u32[]{:S(2)}, u32[]{:S(2)}) collective-permute-start(bf16[128,2,128]{2,0,1:T(8,128)(2,1)S(1)} %copy.87), channel_id=1, source_target_pairs={{0,4},{4,8},{8,12},{1,5},{5,9},{9,13},{2,6},{6,10},{10,14},{3,7},{... | collective-permute-start | bytes 196616 | tf_op jit(solution)/shard_map/ppermute | solution.py:15
  10.5 48.5 %collective-permute-start.1 = (bf16[128,2,128]{2,0,1:T(8,128)(2,1)S(1)}, bf16[128,2,128]{2,0,1:T(8,128)(2,1)}, u32[]{:S(2)}, u32[]{:S(2)}) collective-permute-start(bf16[128,2,128]{2,0,1:T(8,128)(2,1)S(1)} %copy.88), channel_id=1, source_target_pairs={{0,4},{4,8},{8,12},{1,5},{5,9},{9,13},{2,6},{6,10},{10,14},{3,7},{... | collective-permute-start | bytes 196616 | tf_op jit(solution)/shard_map/ppermute | solution.py:15
  17.5 30.4 %copy-start.3 = (s32[1,6]{1,0:T(1,128)S(1)}, s32[1,6]{1,0:T(1,128)}, u32[]{:S(2)}) copy-start(s32[1,6]{1,0:T(1,128)} %param.23) | copy-start | bytes 76
  48.1 11.8 %copy-start.4 = (s32[1,2]{1,0:T(1,128)S(1)}, s32[1,2]{1,0:T(1,128)}, u32[]{:S(2)}) copy-start(s32[1,2]{1,0:T(1,128)} %param.24) | copy-start | bytes 28
  48.3 2.2 %copy-start.1 = (bf16[8,128,2,128]{3,2,1,0:T(2,128)(2,1)}, bf16[8,128,2,128]{3,2,1,0:T(2,128)(2,1)S(1)}, u32[]{:S(2)}) copy-start(bf16[8,128,2,128]{3,2,1,0:T(2,128)(2,1)S(1)} %get-tuple-element.517) | copy-start | bytes 1572868 | tf_op jit(solution)/shard_map/while
  56.7 2.2 %copy-start.2 = (bf16[8,128,2,128]{3,2,1,0:T(2,128)(2,1)S(1)}, bf16[8,128,2,128]{3,2,1,0:T(2,128)(2,1)}, u32[]{:S(2)}) copy-start(bf16[8,128,2,128]{3,2,1,0:T(2,128)(2,1)} %copy-done.1) | copy-start | bytes 1572868 | tf_op jit(solution)/shard_map/while
where the time goes:
time: 81.5 us; the launch traced here: 81 us
  blocking collectives  33.8 us (41%)
  local copies, waits for them, and re-layouts  17 us (21%)
  starting transfers between devices  10.6 us (13%)
  other arithmetic  6.58 us (8%)
  loops' own time  6.47 us (8%)
  matrix products  5.18 us (6%)
  between operations  1.4 us (2%)
    all_gather x1, blocking collectives, shards(): lax.all_gather(chosen_keys, 'ctx', axis=0, tiled=True)  11.9 us
    all_gather x1, blocking collectives, shards(): lax.all_gather(chosen_values, 'ctx', axis=0, tiled=True)  11.8 us
    all_to_all x1, blocking collectives, shards(): lax.all_to_all(attention, 'sub', split_axis=2, concat_axis=1, tiled=True)  10.2 us
    ppermute x2, starting transfers between devices, from_behind(): return lax.ppermute(block, axis, route)  6.41 us
    another operation x1, loops' own time, slash_range(): return lax.fori_loop(0, entry_count, slash_step, carry_state)  6.16 us
    all_to_all x1, starting transfers between devices, shards(): lax.all_to_all(queries, 'sub', split_axis=1, concat_axis=2, tiled=True)  4.15 us
    dynamic_slice x1, local copies, waits for them, and re-layouts, shards(): lax.dynamic_slice_in_dim(cache_values, first_head, kv_width, 1)  3.75 us
    dot_general x3, matrix products, block_update(): jnp.einsum('rkgc,ckd->rkgd', weights.astype(jnp.bfloat16), block_values,...  3.28 us
  transfers between devices with their start and end apart: 3, of which 0 were waited for; matrix products, arithmetic and copies ran while one was open for 26% of the time, Pallas kernels for 0%

commit v1 on v0

v1 whole, which is shorter than its diff:
```python
import functools
import math

import jax
import jax.numpy as jnp
from jax import lax
from jax.experimental import pallas as pl
from jax.experimental.pallas import tpu as pltpu
from jax.sharding import PartitionSpec as P

BLK = 128
MESH = pl.DeviceIdType.MESH


def attend(n, q_ref, own_ref, new_ref, vl_ref, sl_ref, cnt_ref, o_ref,
           pool, slash, acc, peak, total,
           hop_send, hop_recv, sib_send, sib_recv, sl_sem):
    z = lax.axis_index("ctx")
    s = lax.axis_index("sub")
    heads, rows, head_dim = q_ref.shape
    groups = rows // BLK
    c = math.log2(math.e) / math.sqrt(head_dim)
    has_left = z > 0
    has_right = z < n - 1
    sib_id = {"sub": 1 - s}

    barrier = pltpu.get_barrier_semaphore()
    pl.semaphore_signal(barrier, inc=1, device_id=sib_id, device_id_type=MESH)

    @pl.when(has_left)
    def _():
        pl.semaphore_signal(barrier, inc=1, device_id={"ctx": z - 1}, device_id_type=MESH)

    @pl.when(has_right)
    def _():
        pl.semaphore_signal(barrier, inc=1, device_id={"ctx": z + 1}, device_id_type=MESH)

    pl.semaphore_wait(barrier, 1 + has_left.astype(jnp.int32) + has_right.astype(jnp.int32))

    def hop(src_ref, src, kv, right):
        return pltpu.make_async_remote_copy(
            src_ref=src_ref, dst_ref=pool.at[src, s, kv],
            send_sem=hop_send.at[src, int(right), kv], recv_sem=hop_recv.at[src, kv],
            device_id={"ctx": z + 1 if right else z - 1}, device_id_type=MESH)

    def sib(src, kv):
        return pltpu.make_async_remote_copy(
            src_ref=pool.at[src, s, kv], dst_ref=pool.at[src, s, kv],
            send_sem=sib_send.at[src, kv], recv_sem=sib_recv.at[src, kv],
            device_id=sib_id, device_id_type=MESH)

    def sib_in(src, kv):
        return pltpu.make_async_remote_copy(
            src_ref=pool.at[src, 1 - s, kv], dst_ref=pool.at[src, 1 - s, kv],
            send_sem=sib_send.at[src, kv], recv_sem=sib_recv.at[src, kv],
            device_id=sib_id, device_id_type=MESH)

    def slash_hop():
        return pltpu.make_async_remote_copy(
            src_ref=new_ref.at[s], dst_ref=slash.at[s],
            send_sem=sl_sem.at[0], recv_sem=sl_sem.at[1],
            device_id={"ctx": z + 1}, device_id_type=MESH)

    def slash_sib(part):
        return pltpu.make_async_remote_copy(
            src_ref=slash.at[part], dst_ref=slash.at[part],
            send_sem=sl_sem.at[2], recv_sem=sl_sem.at[3],
            device_id=sib_id, device_id_type=MESH)

    @pl.when(has_right)
    def _():
        for kv in range(2):
            hop(own_ref.at[s, kv], z, kv, True).start()

    @pl.when(has_left)
    def _():
        for kv in range(2):
            hop(own_ref.at[s, kv], z, kv, False).start()

    @pl.when((z == 0) & has_right)
    def _():
        slash_hop().start()

    def listed(slot):
        count = cnt_ref[0, 0]
        width = vl_ref.shape[1]
        if width <= 8:
            hit = jnp.int32(0)
            for i in range(width):
                hit = hit | jnp.where((vl_ref[0, i] == slot) & (i < count), 1, 0)
            return hit

        def one(i, hit):
            return hit | jnp.where((vl_ref[0, i] == slot) & (i < count), 1, 0)

        return lax.fori_loop(0, width, one, jnp.int32(0))

    def score(keys, q):
        return lax.dot_general(keys, q, (((1,), (1,)), ((), ())),
                               preferred_element_type=jnp.float32)

    def update(blocks, first=False):
        def one_head(h, carry):
            q = q_ref[h]
            raw = []
            tops = []
            for keys, _, seen in blocks:
                scores = score(keys[h], q)
                if seen is None:
                    key_id = lax.broadcasted_iota(jnp.int32, scores.shape, 0)
                    row_id = lax.broadcasted_iota(jnp.int32, scores.shape, 1) // groups
                    scores = jnp.where(key_id <= row_id, scores, -jnp.inf)
                top = jnp.max(scores, axis=0, keepdims=True)
                if seen is not None:
                    top = jnp.where(seen > 0, top, -jnp.inf)
                raw.append(scores)
                tops.append(top)
            high = functools.reduce(jnp.maximum, tops)
            if not first:
                old = peak[h]
                high = jnp.maximum(old, high)
                factor = jnp.exp2((old - high) * c)
            peak[h] = high
            sums = []
            parts = []
            for (_, values, seen), scores in zip(blocks, raw):
                base = high if seen is None else jnp.where(seen > 0, high, jnp.inf)
                weights = jnp.exp2((scores - base) * c)
                sums.append(jnp.sum(weights, axis=0, keepdims=True))
                parts.append(jnp.dot(values[h], weights.astype(jnp.bfloat16),
                                     preferred_element_type=jnp.float32))
            add_total = sum(sums[1:], sums[0])
            add_acc = sum(parts[1:], parts[0])
            if first:
                total[h] = add_total
                acc[h] = add_acc
            else:
                total[h] = total[h] * factor + add_total
                acc[h] = acc[h] * factor + add_acc
            return carry

        lax.fori_loop(0, heads, one_head, 0)

    update([(new_ref.at[0], new_ref.at[1], None)]
           + [(own_ref.at[b, 0], own_ref.at[b, 1], listed(2 * z + b)) for b in range(2)],
           first=True)

    def pool_update(src):
        update([(pool.at[src, b, 0], pool.at[src, b, 1], listed(2 * src + b))
                for b in range(2)])

    def step(d, carry):
        lo = z - d
        hi = z + d
        for kv in range(2):
            @pl.when(lo >= 0)
            def _():
                hop(own_ref.at[s, kv], lo, kv, True).wait_recv()

                @pl.when(has_right)
                def _():
                    hop(pool.at[lo, s, kv], lo, kv, True).start()

                sib(lo, kv).start()

            @pl.when(hi < n)
            def _():
                hop(own_ref.at[s, kv], hi, kv, False).wait_recv()

                @pl.when(has_left)
                def _():
                    hop(pool.at[hi, s, kv], hi, kv, False).start()

                sib(hi, kv).start()

        @pl.when((d == z) & has_right)
        def _():
            slash_hop().start()

        @pl.when(lo >= 0)
        def _():
            for kv in range(2):
                sib_in(lo, kv).wait_recv()
            pool_update(lo)

        @pl.when(hi < n)
        def _():
            for kv in range(2):
                sib_in(hi, kv).wait_recv()
            pool_update(hi)

        return carry

    lax.fori_loop(1, n, step, 0)

    @pl.when(has_left)
    def _():
        slash_hop().wait_recv()
        slash_sib(s).start()
        slash_sib(1 - s).wait_recv()
        back = jnp.int32(0)
        for i in range(sl_ref.shape[1]):
            back = back | jnp.where((sl_ref[0, i] == 1) & (i < cnt_ref[0, 1]), 1, 0)
        update([(slash.at[0], slash.at[1], back)])
        slash_sib(s).wait_send()

    def finish(h, carry):
        o_ref[h] = jnp.transpose(acc[h] / total[h]).astype(o_ref.dtype)
        return carry

    lax.fori_loop(0, heads, finish, 0)

    def drain(src, carry):
        for kv in range(2):
            @pl.when(has_right & (src <= z))
            def _():
                hop(own_ref.at[s, kv], src, kv, True).wait_send()

            @pl.when(has_left & (src >= z))
            def _():
                hop(own_ref.at[s, kv], src, kv, False).wait_send()

            @pl.when(src != z)
            def _():
                sib(src, kv).wait_send()
        return carry

    lax.fori_loop(0, n, drain, 0)

    @pl.when(has_right)
    def _():
        slash_hop().wait_send()


def shards(n, queries, new_keys, new_values, cache_keys, cache_values,
           vertical_pool, vertical_lists, slash_lists, list_counts):
    tokens, heads, groups, head_dim = queries.shape
    rows = tokens * groups
    picked = vertical_pool.shape[0]

    def pick(cache, order):
        return jnp.stack([
            lax.dynamic_slice_in_dim(cache, vertical_pool[i] * BLK, BLK, 0).transpose(order)
            for i in range(picked)])

    own = jnp.stack([pick(cache_keys, (1, 0, 2)), pick(cache_values, (1, 2, 0))], 1)
    new = jnp.stack([new_keys.transpose(1, 0, 2), new_values.transpose(1, 2, 0)])
    q = queries.transpose(1, 0, 2, 3).reshape(heads, rows, head_dim)
    vmem = pl.BlockSpec(memory_space=pltpu.VMEM)
    smem = pl.BlockSpec(memory_space=pltpu.SMEM)
    dma = pltpu.SemaphoreType.DMA
    out = pl.pallas_call(
        functools.partial(attend, n),
        out_shape=jax.ShapeDtypeStruct((heads, rows, head_dim), jnp.bfloat16),
        in_specs=[vmem, vmem, vmem, smem, smem, smem],
        out_specs=vmem,
        scratch_shapes=[
            pltpu.VMEM((n, picked, 2, heads, BLK, head_dim), jnp.bfloat16),
            pltpu.VMEM((2, heads, BLK, head_dim), jnp.bfloat16),
            pltpu.VMEM((heads, head_dim, rows), jnp.float32),
            pltpu.VMEM((heads, 1, rows), jnp.float32),
            pltpu.VMEM((heads, 1, rows), jnp.float32),
            dma((n, 2, 2)), dma((n, 2)), dma((n, 2)), dma((n, 2)), dma((4,)),
        ],
        compiler_params=pltpu.CompilerParams(
            collective_id=0, has_side_effects=True, vmem_limit_bytes=60 * 2**20),
    )(q, own, new, vertical_lists, slash_lists, list_counts)
    return out.reshape(heads, tokens, groups, head_dim).transpose(1, 0, 2, 3)


def solution(mesh):
    in_specs = (
        P(("grp", "ctx"), "kvh", "sub", None),
        P(("grp", "ctx"), "kvh", None),
        P(("grp", "ctx"), "kvh", None),
        P(("grp", "ctx"), "kvh", None),
        P(("grp", "ctx"), "kvh", None),
        P(("grp", "ctx")),
        P(("grp", "ctx"), None),
        P(("grp", "ctx"), None),
        P(("grp", "ctx"), None),
    )
    out_specs = P(("grp", "ctx"), "kvh", "sub", None)
    return jax.shard_map(functools.partial(shards, mesh.shape["ctx"]), mesh=mesh,
                         in_specs=in_specs, out_specs=out_specs, check_vma=False)
```

time: 81.5 us -> 41.9 us (0.51)
  the two profiles are of different devices: /device:TPU:11 before, /device:TPU:25 now
where the time goes in v1:
time: 41.9 us; the launch traced here: 41.6 us
  Pallas kernels  30.7 us (73%)
  local copies, waits for them, and re-layouts  7.98 us (19%)
  other arithmetic  1.63 us (4%)
  between operations  1.36 us (3%)
    pallas_call x1, Pallas kernels, shards(): pl.pallas_call(functools.partial(attend, n), out_shape=jax.ShapeDtypeStru...  30.7 us
    unnamed x8, local copies, waits for them, and re-layouts  2.28 us
    reshape x1, local copies, waits for them, and re-layouts, shards(): return out.reshape(heads, tokens, groups, head_dim).transpose(1, 0, 2, 3)  2.02 us
    slice x1, local copies, waits for them, and re-layouts, pick(): vertical_pool[i] * BLK  1.38 us
    dynamic_slice x1, local copies, waits for them, and re-layouts, pick(): lax.dynamic_slice_in_dim(cache, vertical_pool[i] * BLK, BLK, 0)  1.33 us
    transpose x1, local copies, waits for them, and re-layouts, shards(): q = queries.transpose(1, 0, 2, 3).reshape(heads, rows, head_dim)  0.97 us
    another operation x3, other arithmetic, shards(): jnp.stack([pick(cache_keys, (1, 0, 2)), pick(cache_values, (1, 2, 0))], 1)  0.89 us

profile of v1, /device:TPU:25, one launch (start us, length us, event | category | flops | bytes accessed | tf_op | source)
XLA Modules:
  0.0 41.6 jit_solution(8528367109126884238)
XLA Ops:
  0.0 1.4 %fusion = (s32[1]{0:T(128)}, s32[1]{0:T(128)}) fusion(s32[2]{0:T(128)} %param.14), kind=kLoop, calls=%fused_computation.12 | loop fusion | bytes 16 | tf_op jit(solution)/shard_map/slice | solution.py:243
  2.7 0.9 %copy.29 = bf16[128,4,128]{2,0,1:T(8,128)(2,1)S(1)} copy(bf16[128,4,128]{2,1,0:T(4,128)(2,1)} %param.10) | data formatting | bytes 262144 | tf_op args[1]
  3.6 1.0 %copy.16 = bf16[128,4,128]{0,2,1:T(8,128)(2,1)S(1)} copy(bf16[128,4,128]{2,1,0:T(4,128)(2,1)} %param.11) | data formatting | bytes 262144 | tf_op args[2]
  4.6 0.7 %pad_maximum_fusion.1.new_ref = bf16[2,4,128,128]{3,2,1,0:T(8,128)(2,1)} fusion(bf16[1,4,128,128]{3,2,1,0:T(8,128)(2,1)S(1)} %bitcast.44, bf16[1,4,128,128]{3,2,1,0:T(8,128)(2,1)S(1)} %bitcast.43), kind=kLoop, calls=%fused_computation.4 | loop fusion | flops 131072 | bytes 524288 | tf_op jit(solution)/shard_map/stack | solution.py:247
  5.4 0.0 copy-start
  5.4 1.3 %constant_dynamic-slice_fusion.1 = (bf16[128,4,128]{2,1,0:T(4,128)(2,1)S(1)}, bf16[128,4,128]{2,1,0:T(4,128)(2,1)S(1)}, bf16[128,4,128]{2,1,0:T(4,128)(2,1)S(1)}, bf16[128,4,128]{2,1,0:T(4,128)(2,1)S(1)}) fusion(bf16[2048,4,128]{2,1,0:T(4,128)(2,1)} %param.13, s32[]{:T(128)S(6)} %select_n.8, s32[]{:T(128)S(6)} %select_n.9, bf16[2048,4,128]{2,1,0:T(4,128)(2,1)} %param.12), kind=kLoop, calls=%fused_computation.9 | loop fusion | bytes 1048584 | tf_op jit(solution)/shard_map/dynamic_slice | solution.py:243
  6.7 0.1 copy.20
  6.9 0.1 copy.21
  7.1 0.8 %pad_maximum_fusion.own_ref = bf16[2,2,4,128,128]{4,3,2,1,0:T(8,128)(2,1)} fusion(bf16[2,1,4,128,128]{4,3,2,1,0:T(8,128)(2,1)S(1)} %maximum_bitcast_fusion.1, bf16[2,1,4,128,128]{4,3,2,1,0:T(8,128)(2,1)S(1)} %maximum_bitcast_fusion), kind=kLoop, calls=%fused_computation | loop fusion | flops 262144 | bytes 1048576 | tf_op jit(solution)/shard_map/stack | solution.py:246
  8.0 0.0 copy-done
  8.0 1.0 %copy.10 = bf16[4,128,4,128]{3,2,1,0:T(4,128)(2,1)} copy(bf16[4,128,4,128]{3,2,0,1:T(4,128)(2,1)S(1)} %bitcast.38) | data formatting | bytes 1048576 | tf_op jit(solution)/shard_map/transpose | solution.py:248
  8.9 30.7 %shard_map.91 = bf16[4,512,128]{2,1,0:T(8,128)(2,1)} custom-call(bf16[4,512,128]{2,1,0:T(8,128)(2,1)} %bitcast.37, bf16[2,2,4,128,128]{4,3,2,1,0:T(8,128)(2,1)} %pad_maximum_fusion.own_ref, bf16[2,4,128,128]{3,2,1,0:T(8,128)(2,1)} %pad_maximum_fusion.1.new_ref, s32[1,6]{1,0:T(1,128)} %vl_ref.1, s32[1,2]{1,0:T(1,128)} %sl_ref.1, s32[1,2]{1,0:T(1,128)} %cnt_ref.1), custom_call_target="tpu_custom_call" | custom-call | tf_op jit(solution)/shard_map/pallas_call | solution.py:252
  39.6 2.0 %copy.26 = bf16[4,128,4,128]{3,2,0,1:T(4,128)(2,1)} copy(bf16[4,128,4,128]{3,2,1,0:T(4,128)(2,1)} %bitcast.36) | data formatting | bytes 1048576 | tf_op jit(solution)/shard_map/reshape | solution.py:268
  (4 shorter events, 0.1 us)
Async XLA Ops:
  5.4 2.6 %copy-start = (bf16[128,4,4,128]{3,2,1,0:T(4,128)(2,1)S(1)}, bf16[128,4,4,128]{3,2,1,0:T(4,128)(2,1)}, u32[]{:S(2)}) copy-start(bf16[128,4,4,128]{3,2,1,0:T(4,128)(2,1)} %param.9) | copy-start | bytes 1572868

commit v2 on v1

--- a/solution.py
+++ b/solution.py
@@ -12,13 +12,19 @@
 MESH = pl.DeviceIdType.MESH
 
 
-def attend(n, q_ref, own_ref, new_ref, vl_ref, sl_ref, cnt_ref, o_ref,
+def attend(n, q_hbm, nk_hbm, nv_hbm, ck_hbm, cv_hbm, vp_ref, vl_ref, sl_ref, cnt_ref, o_ref,
+           q_raw, nk_raw, nv_raw, ck_raw, cv_raw, q_ref, own_ref, new_ref, sort_kv, sort_q,
            pool, slash, acc, peak, total,
-           hop_send, hop_recv, sib_send, sib_recv, sl_sem):
+           hop_send, hop_recv, sib_send, sib_recv, sl_sem, in_sem):
     z = lax.axis_index("ctx")
     s = lax.axis_index("sub")
     heads, rows, head_dim = q_ref.shape
     groups = rows // BLK
+    wide = heads * BLK
+    loads = [pltpu.make_async_copy(src, dst, in_sem.at[i]) for i, (src, dst) in enumerate(
+        [(ck_hbm, ck_raw), (cv_hbm, cv_raw), (nk_hbm, nk_raw), (nv_hbm, nv_raw), (q_hbm, q_raw)])]
+    for load in loads:
+        load.start()
     c = math.log2(math.e) / math.sqrt(head_dim)
     has_left = z > 0
     has_right = z < n - 1
@@ -35,6 +41,34 @@
     def _():
         pl.semaphore_signal(barrier, inc=1, device_id={"ctx": z + 1}, device_id_type=MESH)
 
+    ids = lax.broadcasted_iota(jnp.int32, (wide, wide), 0)
+    at = lax.broadcasted_iota(jnp.int32, (wide, wide), 1)
+    sort_kv[...] = jnp.where(at == (ids % BLK) * heads + ids // BLK, 1.0, 0.0).astype(jnp.bfloat16)
+    token = (ids % BLK) // groups
+    sort_q[...] = jnp.where(at == (token * heads + ids // BLK) * groups + ids % groups,
+                            1.0, 0.0).astype(jnp.bfloat16)
+
+    def by_head(raw):
+        return jnp.dot(sort_kv[...], raw, preferred_element_type=jnp.float32).astype(jnp.bfloat16)
+
+    def put_keys(dst, raw):
+        ordered = by_head(raw)
+        for h in range(heads):
+            dst[h] = ordered[h * BLK:(h + 1) * BLK]
+
+    def put_values(dst, raw):
+        ordered = lax.dot_general(raw, sort_kv[...], (((0,), (1,)), ((), ())),
+                                  preferred_element_type=jnp.float32).astype(jnp.bfloat16)
+        for h in range(heads):
+            dst[h] = ordered[:, h * BLK:(h + 1) * BLK]
+
+    def chosen(cache, b):
+        return cache[vp_ref[b]]
+
+    loads[0].wait()
+    put_keys(own_ref.at[s, 0], chosen(ck_raw, s))
+    loads[1].wait()
+    put_values(own_ref.at[s, 1], chosen(cv_raw, s))
     pl.semaphore_wait(barrier, 1 + has_left.astype(jnp.int32) + has_right.astype(jnp.int32))
 
     def hop(src_ref, src, kv, right):
@@ -77,9 +111,23 @@
         for kv in range(2):
             hop(own_ref.at[s, kv], z, kv, False).start()
 
+    loads[2].wait()
+    loads[3].wait()
+    put_keys(new_ref.at[0], nk_raw[...])
+    put_values(new_ref.at[1], nv_raw[...])
+
     @pl.when((z == 0) & has_right)
     def _():
         slash_hop().start()
+
+    put_keys(own_ref.at[1 - s, 0], chosen(ck_raw, 1 - s))
+    put_values(own_ref.at[1 - s, 1], chosen(cv_raw, 1 - s))
+    loads[4].wait()
+    for part in range(rows // BLK):
+        ordered = jnp.dot(sort_q[...], q_raw[part * wide:(part + 1) * wide],
+                          preferred_element_type=jnp.float32).astype(jnp.bfloat16)
+        for h in range(heads):
+            q_ref[h, part * BLK:(part + 1) * BLK] = ordered[h * BLK:(h + 1) * BLK]
 
     def listed(slot):
         count = cnt_ref[0, 0]
@@ -100,7 +148,7 @@
                                preferred_element_type=jnp.float32)
 
     def update(blocks, first=False):
-        def one_head(h, carry):
+        def one_head(h):
             q = q_ref[h]
             raw = []
             tops = []
@@ -137,9 +185,9 @@
             else:
                 total[h] = total[h] * factor + add_total
                 acc[h] = acc[h] * factor + add_acc
-            return carry
-
-        lax.fori_loop(0, heads, one_head, 0)
+
+        for h in range(heads):
+            one_head(h)
 
     update([(new_ref.at[0], new_ref.at[1], None)]
            + [(own_ref.at[b, 0], own_ref.at[b, 1], listed(2 * z + b)) for b in range(2)],
@@ -204,11 +252,13 @@
         update([(slash.at[0], slash.at[1], back)])
         slash_sib(s).wait_send()
 
-    def finish(h, carry):
-        o_ref[h] = jnp.transpose(acc[h] / total[h]).astype(o_ref.dtype)
-        return carry
-
-    lax.fori_loop(0, heads, finish, 0)
+    for part in range(rows // BLK):
+        lanes = slice(part * BLK, (part + 1) * BLK)
+        done = jnp.concatenate(
+            [(acc[h, :, lanes] / total[h, :, lanes]).astype(jnp.bfloat16) for h in range(heads)], 1)
+        o_ref[part * wide:(part + 1) * wide] = lax.dot_general(
+            sort_q[...], done, (((0,), (1,)), ((), ())),
+            preferred_element_type=jnp.float32).astype(o_ref.dtype)
 
     def drain(src, carry):
         for kv in range(2):
@@ -238,34 +288,40 @@
     rows = tokens * groups
     picked = vertical_pool.shape[0]
 
-    def pick(cache, order):
-        return jnp.stack([
-            lax.dynamic_slice_in_dim(cache, vertical_pool[i] * BLK, BLK, 0).transpose(order)
-            for i in range(picked)])
-
-    own = jnp.stack([pick(cache_keys, (1, 0, 2)), pick(cache_values, (1, 2, 0))], 1)
-    new = jnp.stack([new_keys.transpose(1, 0, 2), new_values.transpose(1, 2, 0)])
-    q = queries.transpose(1, 0, 2, 3).reshape(heads, rows, head_dim)
-    vmem = pl.BlockSpec(memory_space=pltpu.VMEM)
+    def flat(x):
+        return x.reshape(-1, head_dim)
+
+    def vmem(*shape):
+        return pltpu.VMEM(shape, jnp.bfloat16)
+
+    hbm = pl.BlockSpec(memory_space=pl.ANY)
     smem = pl.BlockSpec(memory_space=pltpu.SMEM)
     dma = pltpu.SemaphoreType.DMA
+    wide = heads * BLK
+    cached = cache_keys.shape[0] // BLK
     out = pl.pallas_call(
         functools.partial(attend, n),
-        out_shape=jax.ShapeDtypeStruct((heads, rows, head_dim), jnp.bfloat16),
-        in_specs=[vmem, vmem, vmem, smem, smem, smem],
-        out_specs=vmem,
+        out_shape=jax.ShapeDtypeStruct((tokens * heads * groups, head_dim), jnp.bfloat16),
+        in_specs=[hbm] * 5 + [smem] * 4,
+        out_specs=pl.BlockSpec(memory_space=pltpu.VMEM),
         scratch_shapes=[
-            pltpu.VMEM((n, picked, 2, heads, BLK, head_dim), jnp.bfloat16),
-            pltpu.VMEM((2, heads, BLK, head_dim), jnp.bfloat16),
+            vmem(heads * rows, head_dim), vmem(wide, head_dim), vmem(wide, head_dim),
+            vmem(cached, wide, head_dim), vmem(cached, wide, head_dim),
+            vmem(heads, rows, head_dim), vmem(picked, 2, heads, BLK, head_dim),
+            vmem(2, heads, BLK, head_dim), vmem(wide, wide), vmem(wide, wide),
+            vmem(n, picked, 2, heads, BLK, head_dim),
+            vmem(2, heads, BLK, head_dim),
             pltpu.VMEM((heads, head_dim, rows), jnp.float32),
             pltpu.VMEM((heads, 1, rows), jnp.float32),
             pltpu.VMEM((heads, 1, rows), jnp.float32),
-            dma((n, 2, 2)), dma((n, 2)), dma((n, 2)), dma((n, 2)), dma((4,)),
+            dma((n, 2, 2)), dma((n, 2)), dma((n, 2)), dma((n, 2)), dma((4,)), dma((5,)),
         ],
         compiler_params=pltpu.CompilerParams(
             collective_id=0, has_side_effects=True, vmem_limit_bytes=60 * 2**20),
-    )(q, own, new, vertical_lists, slash_lists, list_counts)
-    return out.reshape(heads, tokens, groups, head_dim).transpose(1, 0, 2, 3)
+    )(flat(queries), flat(new_keys), flat(new_values), cache_keys.reshape(cached, wide, head_dim),
+      cache_values.reshape(cached, wide, head_dim),
+      vertical_pool, vertical_lists, slash_lists, list_counts)
+    return out.reshape(tokens, heads, groups, head_dim)
 
 
 def solution(mesh):

time: 41.9 us -> 31.8 us (0.76)
  local copies, waits for them, and re-layouts: 7.98 us -> 2.02 us
  other arithmetic: 1.63 us -> 0 us
  between operations: 1.36 us -> 0.01 us
  Pallas kernels: 30.7 us -> 29.6 us
    reshape x1 -> x0, local copies, waits for them, and re-layouts: 2.02 us -> none  [shards(): return out.reshape(heads, tokens, groups, head_dim).transpose(1, 0, 2, 3)]
    another operation x4 -> x0, other arithmetic: 1.63 us -> none  [the longest x3 0.89 us: shards(): jnp.stack([pick(cache_keys, (1, 0, 2)), pick(cache_values, (1, 2, 0))], 1)]
    slice x1 -> x0, local copies, waits for them, and re-layouts: 1.38 us -> none  [pick(): vertical_pool[i] * BLK]
    dynamic_slice x1 -> x0, local copies, waits for them, and re-layouts: 1.33 us -> none  [pick(): lax.dynamic_slice_in_dim(cache, vertical_pool[i] * BLK, BLK, 0)]
    pallas_call x1, Pallas kernels: 30.7 us -> 29.6 us  [shards(): pl.pallas_call(functools.partial(attend, n), out_shape=jax.ShapeDtypeStru...]
    transpose x1 -> x0, local copies, waits for them, and re-layouts: 0.97 us -> none  [shards(): q = queries.transpose(1, 0, 2, 3).reshape(heads, rows, head_dim)]
    unnamed x8 -> x1, local copies, waits for them, and re-layouts: 2.28 us -> 2.02 us
where the time goes in v2:
time: 31.8 us; the launch traced here: 31.6 us
  Pallas kernels  29.6 us (93%)
  local copies, waits for them, and re-layouts  2.02 us (6%)
    pallas_call x1, Pallas kernels, shards(): pl.pallas_call(functools.partial(attend, n), out_shape=jax.ShapeDtypeStru...  29.6 us
    unnamed x1, local copies, waits for them, and re-layouts  2.02 us

profile of v2, /device:TPU:25, one launch (start us, length us, event | category | flops | bytes accessed | tf_op | source)
XLA Modules:
  0.0 31.6 jit_solution(6280631295986552780)
XLA Ops:
  0.0 29.6 %shard_map.91 = bf16[2048,128]{1,0:T(8,128)(2,1)} custom-call(bf16[2048,128]{1,0:T(8,128)(2,1)} %bitcast.9, bf16[512,128]{1,0:T(8,128)(2,1)} %bitcast.10, bf16[512,128]{1,0:T(8,128)(2,1)} %bitcast.11, bf16[16,512,128]{2,1,0:T(8,128)(2,1)} %bitcast.6, bf16[16,512,128]{2,1,0:T(8,128)(2,1)} %bitcast.7, s32[2]{0:T(128)} %vp_ref.1, s32[1,6]{1,0:T(1,128)} %vl_ref.1, ...), custom_call_target="tpu_custom_call" | custom-call | tf_op jit(solution)/shard_map/pallas_call | solution.py:302
  29.6 2.0 %copy.11 = bf16[128,4,4,128]{3,2,1,0:T(4,128)(2,1)} copy(bf16[128,4,4,128]{3,2,1,0:T(4,128)(2,1)} %bitcast.8) | data formatting | bytes 1048576

commit v3 on v2

--- a/solution.py
+++ b/solution.py
@@ -14,7 +14,7 @@
 
 def attend(n, q_hbm, nk_hbm, nv_hbm, ck_hbm, cv_hbm, vp_ref, vl_ref, sl_ref, cnt_ref, o_ref,
            q_raw, nk_raw, nv_raw, ck_raw, cv_raw, q_ref, own_ref, new_ref, sort_kv, sort_q,
-           pool, slash, acc, peak, total,
+           pool, slash_raw, slash, acc, peak, total, rounded, fade,
            hop_send, hop_recv, sib_send, sib_recv, sl_sem, in_sem):
     z = lax.axis_index("ctx")
     s = lax.axis_index("sub")
@@ -23,8 +23,8 @@
     wide = heads * BLK
     loads = [pltpu.make_async_copy(src, dst, in_sem.at[i]) for i, (src, dst) in enumerate(
         [(ck_hbm, ck_raw), (cv_hbm, cv_raw), (nk_hbm, nk_raw), (nv_hbm, nv_raw), (q_hbm, q_raw)])]
-    for load in loads:
-        load.start()
+    loads[0].start()
+    loads[1].start()
     c = math.log2(math.e) / math.sqrt(head_dim)
     has_left = z > 0
     has_right = z < n - 1
@@ -65,10 +65,6 @@
     def chosen(cache, b):
         return cache[vp_ref[b]]
 
-    loads[0].wait()
-    put_keys(own_ref.at[s, 0], chosen(ck_raw, s))
-    loads[1].wait()
-    put_values(own_ref.at[s, 1], chosen(cv_raw, s))
     pl.semaphore_wait(barrier, 1 + has_left.astype(jnp.int32) + has_right.astype(jnp.int32))
 
     def hop(src_ref, src, kv, right):
@@ -89,37 +85,44 @@
             send_sem=sib_send.at[src, kv], recv_sem=sib_recv.at[src, kv],
             device_id=sib_id, device_id_type=MESH)
 
-    def slash_hop():
-        return pltpu.make_async_remote_copy(
-            src_ref=new_ref.at[s], dst_ref=slash.at[s],
+    def slash_hop(src_ref=nk_hbm):
+        return pltpu.make_async_remote_copy(
+            src_ref=src_ref, dst_ref=slash_raw.at[s],
             send_sem=sl_sem.at[0], recv_sem=sl_sem.at[1],
             device_id={"ctx": z + 1}, device_id_type=MESH)
 
     def slash_sib(part):
         return pltpu.make_async_remote_copy(
-            src_ref=slash.at[part], dst_ref=slash.at[part],
+            src_ref=slash_raw.at[part], dst_ref=slash_raw.at[part],
             send_sem=sl_sem.at[2], recv_sem=sl_sem.at[3],
             device_id=sib_id, device_id_type=MESH)
 
-    @pl.when(has_right)
-    def _():
-        for kv in range(2):
+    for part, src_ref in enumerate((nk_hbm, nv_hbm)):
+        @pl.when(has_right & (s == part))
+        def _():
+            slash_hop(src_ref).start()
+
+    def send_own(kv):
+        @pl.when(has_right)
+        def _():
             hop(own_ref.at[s, kv], z, kv, True).start()
 
-    @pl.when(has_left)
-    def _():
-        for kv in range(2):
+        @pl.when(has_left)
+        def _():
             hop(own_ref.at[s, kv], z, kv, False).start()
 
+    loads[0].wait()
+    put_keys(own_ref.at[s, 0], chosen(ck_raw, s))
+    for load in loads[2:]:
+        load.start()
+    send_own(0)
+    loads[1].wait()
+    put_values(own_ref.at[s, 1], chosen(cv_raw, s))
+    send_own(1)
     loads[2].wait()
     loads[3].wait()
     put_keys(new_ref.at[0], nk_raw[...])
     put_values(new_ref.at[1], nv_raw[...])
-
-    @pl.when((z == 0) & has_right)
-    def _():
-        slash_hop().start()
-
     put_keys(own_ref.at[1 - s, 0], chosen(ck_raw, 1 - s))
     put_values(own_ref.at[1 - s, 1], chosen(cv_raw, 1 - s))
     loads[4].wait()
@@ -147,12 +150,12 @@
         return lax.dot_general(keys, q, (((1,), (1,)), ((), ())),
                                preferred_element_type=jnp.float32)
 
-    def update(blocks, first=False):
-        def one_head(h):
+    def take_keys(side, blocks, first=False):
+        for h in range(heads):
             q = q_ref[h]
             raw = []
             tops = []
-            for keys, _, seen in blocks:
+            for keys, seen in blocks:
                 scores = score(keys[h], q)
                 if seen is None:
                     key_id = lax.broadcasted_iota(jnp.int32, scores.shape, 0)
@@ -168,89 +171,75 @@
                 old = peak[h]
                 high = jnp.maximum(old, high)
                 factor = jnp.exp2((old - high) * c)
+                fade[side, h] = factor
             peak[h] = high
             sums = []
-            parts = []
-            for (_, values, seen), scores in zip(blocks, raw):
+            for i, ((_, seen), scores) in enumerate(zip(blocks, raw)):
                 base = high if seen is None else jnp.where(seen > 0, high, jnp.inf)
                 weights = jnp.exp2((scores - base) * c)
                 sums.append(jnp.sum(weights, axis=0, keepdims=True))
-                parts.append(jnp.dot(values[h], weights.astype(jnp.bfloat16),
-                                     preferred_element_type=jnp.float32))
-            add_total = sum(sums[1:], sums[0])
-            add_acc = sum(parts[1:], parts[0])
-            if first:
-                total[h] = add_total
-                acc[h] = add_acc
-            else:
-                total[h] = total[h] * factor + add_total
-                acc[h] = acc[h] * factor + add_acc
-
-        for h in range(heads):
-            one_head(h)
-
-    update([(new_ref.at[0], new_ref.at[1], None)]
-           + [(own_ref.at[b, 0], own_ref.at[b, 1], listed(2 * z + b)) for b in range(2)],
-           first=True)
-
-    def pool_update(src):
-        update([(pool.at[src, b, 0], pool.at[src, b, 1], listed(2 * src + b))
-                for b in range(2)])
-
-    def step(d, carry):
-        lo = z - d
-        hi = z + d
-        for kv in range(2):
-            @pl.when(lo >= 0)
-            def _():
-                hop(own_ref.at[s, kv], lo, kv, True).wait_recv()
-
-                @pl.when(has_right)
-                def _():
-                    hop(pool.at[lo, s, kv], lo, kv, True).start()
-
-                sib(lo, kv).start()
-
-            @pl.when(hi < n)
-            def _():
-                hop(own_ref.at[s, kv], hi, kv, False).wait_recv()
-
-                @pl.when(has_left)
-                def _():
-                    hop(pool.at[hi, s, kv], hi, kv, False).start()
-
-                sib(hi, kv).start()
-
-        @pl.when((d == z) & has_right)
-        def _():
-            slash_hop().start()
-
-        @pl.when(lo >= 0)
-        def _():
-            for kv in range(2):
-                sib_in(lo, kv).wait_recv()
-            pool_update(lo)
-
-        @pl.when(hi < n)
-        def _():
-            for kv in range(2):
-                sib_in(hi, kv).wait_recv()
-            pool_update(hi)
-
-        return carry
-
-    lax.fori_loop(1, n, step, 0)
+                rounded[side, h, i * BLK:(i + 1) * BLK] = weights.astype(jnp.bfloat16)
+            add = sum(sums[1:], sums[0])
+            total[h] = add if first else total[h] * fade[side, h] + add
+
+    def take_values(side, blocks, first=False):
+        depth = len(blocks) * BLK
+        for h in range(heads):
+            values = jnp.concatenate([values[h] for values in blocks], 1)
+            add = jnp.dot(values, rounded[side, h, :depth], preferred_element_type=jnp.float32)
+            acc[h] = add if first else acc[h] * fade[side, h] + add
+
+    take_keys(0, [(new_ref.at[0], None)]
+              + [(own_ref.at[b, 0], listed(2 * z + b)) for b in range(2)], first=True)
+    take_values(0, [new_ref.at[1]] + [own_ref.at[b, 1] for b in range(2)], first=True)
 
     @pl.when(has_left)
     def _():
         slash_hop().wait_recv()
         slash_sib(s).start()
-        slash_sib(1 - s).wait_recv()
-        back = jnp.int32(0)
-        for i in range(sl_ref.shape[1]):
-            back = back | jnp.where((sl_ref[0, i] == 1) & (i < cnt_ref[0, 1]), 1, 0)
-        update([(slash.at[0], slash.at[1], back)])
-        slash_sib(s).wait_send()
+
+    def arrive(src, kv, right):
+        hop(own_ref.at[s, kv], src, kv, right).wait_recv()
+
+        @pl.when(has_right if right else has_left)
+        def _():
+            hop(pool.at[src, s, kv], src, kv, right).start()
+
+        sib(src, kv).start()
+
+    def step(d, carry):
+        sides = ((z - d, z - d >= 0, True), (z + d, z + d < n, False))
+        for kv in range(2):
+            for src, there, right in sides:
+                @pl.when(there)
+                def _():
+                    arrive(src, kv, right)
+
+            if kv == 0:
+                @pl.when((d == 1) & has_left)
+                def _():
+                    slash_sib(1 - s).wait_recv()
+                    put_keys(slash.at[0], slash_raw[0])
+                    put_values(slash.at[1], slash_raw[1])
+                    back = jnp.int32(0)
+                    for i in range(sl_ref.shape[1]):
+                        back = back | jnp.where((sl_ref[0, i] == 1) & (i < cnt_ref[0, 1]), 1, 0)
+                    take_keys(0, [(slash.at[0], back)])
+                    take_values(0, [slash.at[1]])
+
+            for side, (src, there, right) in enumerate(sides):
+                @pl.when(there)
+                def _():
+                    sib_in(src, kv).wait_recv()
+                    if kv == 0:
+                        take_keys(side, [(pool.at[src, b, 0], listed(2 * src + b))
+                                         for b in range(2)])
+                    else:
+                        take_values(side, [pool.at[src, b, 1] for b in range(2)])
+
+        return carry
+
+    lax.fori_loop(1, n, step, 0)
 
     for part in range(rows // BLK):
         lanes = slice(part * BLK, (part + 1) * BLK)
@@ -280,6 +269,10 @@
     @pl.when(has_right)
     def _():
         slash_hop().wait_send()
+
+    @pl.when(has_left)
+    def _():
+        slash_sib(s).wait_send()
 
 
 def shards(n, queries, new_keys, new_values, cache_keys, cache_values,
@@ -310,10 +303,11 @@
             vmem(heads, rows, head_dim), vmem(picked, 2, heads, BLK, head_dim),
             vmem(2, heads, BLK, head_dim), vmem(wide, wide), vmem(wide, wide),
             vmem(n, picked, 2, heads, BLK, head_dim),
-            vmem(2, heads, BLK, head_dim),
+            vmem(2, wide, head_dim), vmem(2, heads, BLK, head_dim),
             pltpu.VMEM((heads, head_dim, rows), jnp.float32),
             pltpu.VMEM((heads, 1, rows), jnp.float32),
             pltpu.VMEM((heads, 1, rows), jnp.float32),
+            vmem(2, heads, 3 * BLK, rows), pltpu.VMEM((2, heads, 1, rows), jnp.float32),
             dma((n, 2, 2)), dma((n, 2)), dma((n, 2)), dma((n, 2)), dma((4,)), dma((5,)),
         ],
         compiler_params=pltpu.CompilerParams(

time: 31.8 us -> 30.8 us (0.969)
  the two profiles are of different devices: /device:TPU:25 before, /device:TPU:1 now
where the time goes in v3:
time: 30.8 us; the launch traced here: 30.6 us
  Pallas kernels  28.6 us (93%)
  local copies, waits for them, and re-layouts  2.02 us (7%)
    pallas_call x1, Pallas kernels, shards(): pl.pallas_call(functools.partial(attend, n), out_shape=jax.ShapeDtypeStru...  28.6 us
    unnamed x1, local copies, waits for them, and re-layouts  2.02 us

profile of v3, /device:TPU:1, one launch (start us, length us, event | category | flops | bytes accessed | tf_op | source)
XLA Modules:
  0.0 30.6 jit_solution(3596740465011438886)
XLA Ops:
  0.0 28.6 %shard_map.91 = bf16[2048,128]{1,0:T(8,128)(2,1)} custom-call(bf16[2048,128]{1,0:T(8,128)(2,1)} %bitcast.9, bf16[512,128]{1,0:T(8,128)(2,1)} %bitcast.10, bf16[512,128]{1,0:T(8,128)(2,1)} %bitcast.11, bf16[16,512,128]{2,1,0:T(8,128)(2,1)} %bitcast.6, bf16[16,512,128]{2,1,0:T(8,128)(2,1)} %bitcast.7, s32[2]{0:T(128)} %vp_ref.1, s32[1,6]{1,0:T(1,128)} %vl_ref.1, ...), custom_call_target="tpu_custom_call" | custom-call | tf_op jit(solution)/shard_map/pallas_call | solution.py:295
  28.6 2.0 %copy.11 = bf16[128,4,4,128]{3,2,1,0:T(4,128)(2,1)} copy(bf16[128,4,4,128]{3,2,1,0:T(4,128)(2,1)} %bitcast.8) | data formatting | bytes 1048576

commit v4 on v3

--- a/solution.py
+++ b/solution.py
@@ -24,7 +24,6 @@
     loads = [pltpu.make_async_copy(src, dst, in_sem.at[i]) for i, (src, dst) in enumerate(
         [(ck_hbm, ck_raw), (cv_hbm, cv_raw), (nk_hbm, nk_raw), (nv_hbm, nv_raw), (q_hbm, q_raw)])]
     loads[0].start()
-    loads[1].start()
     c = math.log2(math.e) / math.sqrt(head_dim)
     has_left = z > 0
     has_right = z < n - 1
@@ -112,6 +111,7 @@
             hop(own_ref.at[s, kv], z, kv, False).start()
 
     loads[0].wait()
+    loads[1].start()
     put_keys(own_ref.at[s, 0], chosen(ck_raw, s))
     for load in loads[2:]:
         load.start()
@@ -208,24 +208,12 @@
         sib(src, kv).start()
 
     def step(d, carry):
-        sides = ((z - d, z - d >= 0, True), (z + d, z + d < n, False))
+        sides = ((z + d, z + d < n, False), (z - d, z - d >= 0, True))
         for kv in range(2):
             for src, there, right in sides:
                 @pl.when(there)
                 def _():
                     arrive(src, kv, right)
-
-            if kv == 0:
-                @pl.when((d == 1) & has_left)
-                def _():
-                    slash_sib(1 - s).wait_recv()
-                    put_keys(slash.at[0], slash_raw[0])
-                    put_values(slash.at[1], slash_raw[1])
-                    back = jnp.int32(0)
-                    for i in range(sl_ref.shape[1]):
-                        back = back | jnp.where((sl_ref[0, i] == 1) & (i < cnt_ref[0, 1]), 1, 0)
-                    take_keys(0, [(slash.at[0], back)])
-                    take_values(0, [slash.at[1]])
 
             for side, (src, there, right) in enumerate(sides):
                 @pl.when(there)
@@ -237,17 +225,25 @@
                     else:
                         take_values(side, [pool.at[src, b, 1] for b in range(2)])
 
+        @pl.when((d == 1) & has_left)
+        def _():
+            slash_sib(1 - s).wait_recv()
+            put_keys(slash.at[0], slash_raw[0])
+            put_values(slash.at[1], slash_raw[1])
+            back = jnp.int32(0)
+            for i in range(sl_ref.shape[1]):
+                back = back | jnp.where((sl_ref[0, i] == 1) & (i < cnt_ref[0, 1]), 1, 0)
+            take_keys(0, [(slash.at[0], back)])
+            take_values(0, [slash.at[1]])
+
         return carry
 
     lax.fori_loop(1, n, step, 0)
 
-    for part in range(rows // BLK):
-        lanes = slice(part * BLK, (part + 1) * BLK)
-        done = jnp.concatenate(
-            [(acc[h, :, lanes] / total[h, :, lanes]).astype(jnp.bfloat16) for h in range(heads)], 1)
-        o_ref[part * wide:(part + 1) * wide] = lax.dot_general(
-            sort_q[...], done, (((0,), (1,)), ((), ())),
-            preferred_element_type=jnp.float32).astype(o_ref.dtype)
+    for h in range(heads):
+        done = (acc[h] / total[h]).astype(jnp.bfloat16)
+        for part in range(rows // BLK):
+            o_ref[part, :, h * BLK:(h + 1) * BLK] = done[:, part * BLK:(part + 1) * BLK]
 
     def drain(src, carry):
         for kv in range(2):
@@ -275,6 +271,31 @@
         slash_sib(s).wait_send()
 
 
+def restore(heads, groups, x_hbm, o_hbm, x_ref, staged, in_sem, sem):
+    parts, _, wide = x_ref.shape
+    loads = [pltpu.make_async_copy(x_hbm.at[part], x_ref.at[part], in_sem.at[part])
+             for part in range(parts)]
+    for load in loads:
+        load.start()
+    ids = lax.broadcasted_iota(jnp.int32, (wide, wide), 1)
+    at = lax.broadcasted_iota(jnp.int32, (wide, wide), 0)
+    token = (ids % BLK) // groups
+    unsort = jnp.where(at == (token * heads + ids // BLK) * groups + ids % groups,
+                       1.0, 0.0).astype(jnp.bfloat16)
+    copies = []
+    for part in range(parts):
+        loads[part].wait()
+        staged[part] = lax.dot_general(
+            unsort, x_ref[part], (((1,), (1,)), ((), ())),
+            preferred_element_type=jnp.float32).astype(jnp.bfloat16)
+        copy = pltpu.make_async_copy(
+            staged.at[part], o_hbm.at[pl.ds(part * wide, wide)], sem.at[part])
+        copy.start()
+        copies.append(copy)
+    for copy in copies:
+        copy.wait()
+
+
 def shards(n, queries, new_keys, new_values, cache_keys, cache_values,
            vertical_pool, vertical_lists, slash_lists, list_counts):
     tokens, heads, groups, head_dim = queries.shape
@@ -287,14 +308,15 @@
     def vmem(*shape):
         return pltpu.VMEM(shape, jnp.bfloat16)
 
-    hbm = pl.BlockSpec(memory_space=pl.ANY)
+    hbm = pl.BlockSpec(memory_space=pltpu.HBM)
     smem = pl.BlockSpec(memory_space=pltpu.SMEM)
     dma = pltpu.SemaphoreType.DMA
     wide = heads * BLK
     cached = cache_keys.shape[0] // BLK
+    parts = rows // BLK
     out = pl.pallas_call(
         functools.partial(attend, n),
-        out_shape=jax.ShapeDtypeStruct((tokens * heads * groups, head_dim), jnp.bfloat16),
+        out_shape=jax.ShapeDtypeStruct((parts, head_dim, wide), jnp.bfloat16),
         in_specs=[hbm] * 5 + [smem] * 4,
         out_specs=pl.BlockSpec(memory_space=pltpu.VMEM),
         scratch_shapes=[
@@ -315,7 +337,16 @@
     )(flat(queries), flat(new_keys), flat(new_values), cache_keys.reshape(cached, wide, head_dim),
       cache_values.reshape(cached, wide, head_dim),
       vertical_pool, vertical_lists, slash_lists, list_counts)
-    return out.reshape(tokens, heads, groups, head_dim)
+    flat_out = pl.pallas_call(
+        functools.partial(restore, heads, groups),
+        out_shape=jax.ShapeDtypeStruct((tokens * heads * groups, head_dim), jnp.bfloat16),
+        in_specs=[hbm],
+        out_specs=hbm,
+        scratch_shapes=[vmem(parts, head_dim, wide), vmem(parts, wide, head_dim),
+                        dma((parts,)), dma((parts,))],
+        compiler_params=pltpu.CompilerParams(vmem_limit_bytes=60 * 2**20),
+    )(out)
+    return flat_out.reshape(tokens, heads, groups, head_dim)
 
 
 def solution(mesh):

time: 30.8 us -> 30.6 us (level)
  local copies, waits for them, and re-layouts: 2.02 us -> 0 us
  Pallas kernels: 28.6 us -> 30.4 us
    pallas_call x0 -> x1, Pallas kernels: none -> 3.31 us  [shards(): pl.pallas_call(functools.partial(restore, heads, groups), out_shape=jax.S...]
    unnamed x1 -> x0, local copies, waits for them, and re-layouts: 2.02 us -> none
    pallas_call x1, Pallas kernels: 28.6 us -> 27.1 us  [shards(): pl.pallas_call(functools.partial(attend, n), out_shape=jax.ShapeDtypeStru...]
where the time goes in v4:
time: 30.6 us; the launch traced here: 30.5 us
  Pallas kernels  30.4 us (99%)
    pallas_call x1, Pallas kernels, shards(): pl.pallas_call(functools.partial(attend, n), out_shape=jax.ShapeDtypeStru...  27.1 us
    pallas_call x1, Pallas kernels, shards(): pl.pallas_call(functools.partial(restore, heads, groups), out_shape=jax.S...  3.31 us

profile of v4, /device:TPU:1, one launch (start us, length us, event | category | flops | bytes accessed | tf_op | source)
XLA Modules:
  0.0 30.5 jit_solution(10758498336516990323)
XLA Ops:
  0.0 27.1 %shard_map.91.x_hbm = bf16[4,128,512]{2,1,0:T(8,128)(2,1)} custom-call(bf16[2048,128]{1,0:T(8,128)(2,1)} %bitcast.8, bf16[512,128]{1,0:T(8,128)(2,1)} %bitcast.9, bf16[512,128]{1,0:T(8,128)(2,1)} %bitcast.10, bf16[16,512,128]{2,1,0:T(8,128)(2,1)} %bitcast.6, bf16[16,512,128]{2,1,0:T(8,128)(2,1)} %bitcast.7, s32[2]{0:T(128)} %vp_ref.1, s32[1,6]{1,0:T(1,128)} %vl_ref.1, ...), custom_call_target="tpu_custom_call" | custom-call | tf_op jit(solution)/shard_map/pallas_call | solution.py:317
  27.1 3.3 %shard_map.92 = bf16[2048,128]{1,0:T(8,128)(2,1)} custom-call(bf16[4,128,512]{2,1,0:T(8,128)(2,1)} %shard_map.91.x_hbm), custom_call_target="tpu_custom_call" | custom-call | tf_op jit(solution)/shard_map/pallas_call | solution.py:340

commit v5 on v3

--- a/solution.py
+++ b/solution.py
@@ -24,7 +24,6 @@
     loads = [pltpu.make_async_copy(src, dst, in_sem.at[i]) for i, (src, dst) in enumerate(
         [(ck_hbm, ck_raw), (cv_hbm, cv_raw), (nk_hbm, nk_raw), (nv_hbm, nv_raw), (q_hbm, q_raw)])]
     loads[0].start()
-    loads[1].start()
     c = math.log2(math.e) / math.sqrt(head_dim)
     has_left = z > 0
     has_right = z < n - 1
@@ -112,6 +111,7 @@
             hop(own_ref.at[s, kv], z, kv, False).start()
 
     loads[0].wait()
+    loads[1].start()
     put_keys(own_ref.at[s, 0], chosen(ck_raw, s))
     for load in loads[2:]:
         load.start()
@@ -208,24 +208,12 @@
         sib(src, kv).start()
 
     def step(d, carry):
-        sides = ((z - d, z - d >= 0, True), (z + d, z + d < n, False))
+        sides = ((z + d, z + d < n, False), (z - d, z - d >= 0, True))
         for kv in range(2):
             for src, there, right in sides:
                 @pl.when(there)
                 def _():
                     arrive(src, kv, right)
-
-            if kv == 0:
-                @pl.when((d == 1) & has_left)
-                def _():
-                    slash_sib(1 - s).wait_recv()
-                    put_keys(slash.at[0], slash_raw[0])
-                    put_values(slash.at[1], slash_raw[1])
-                    back = jnp.int32(0)
-                    for i in range(sl_ref.shape[1]):
-                        back = back | jnp.where((sl_ref[0, i] == 1) & (i < cnt_ref[0, 1]), 1, 0)
-                    take_keys(0, [(slash.at[0], back)])
-                    take_values(0, [slash.at[1]])
 
             for side, (src, there, right) in enumerate(sides):
                 @pl.when(there)
@@ -237,6 +225,17 @@
                     else:
                         take_values(side, [pool.at[src, b, 1] for b in range(2)])
 
+        @pl.when((d == 1) & has_left)
+        def _():
+            slash_sib(1 - s).wait_recv()
+            put_keys(slash.at[0], slash_raw[0])
+            put_values(slash.at[1], slash_raw[1])
+            back = jnp.int32(0)
+            for i in range(sl_ref.shape[1]):
+                back = back | jnp.where((sl_ref[0, i] == 1) & (i < cnt_ref[0, 1]), 1, 0)
+            take_keys(0, [(slash.at[0], back)])
+            take_values(0, [slash.at[1]])
+
         return carry
 
     lax.fori_loop(1, n, step, 0)
@@ -287,7 +286,7 @@
     def vmem(*shape):
         return pltpu.VMEM(shape, jnp.bfloat16)
 
-    hbm = pl.BlockSpec(memory_space=pl.ANY)
+    hbm = pl.BlockSpec(memory_space=pltpu.HBM)
     smem = pl.BlockSpec(memory_space=pltpu.SMEM)
     dma = pltpu.SemaphoreType.DMA
     wide = heads * BLK

time: 30.8 us -> 30 us (0.974)
  Pallas kernels: 28.6 us -> 27.8 us
    pallas_call x1, Pallas kernels: 28.6 us -> 27.8 us  [shards(): pl.pallas_call(functools.partial(attend, n), out_shape=jax.ShapeDtypeStru...]
where the time goes in v5:
time: 30 us; the launch traced here: 29.8 us
  Pallas kernels  27.8 us (93%)
  local copies, waits for them, and re-layouts  2.02 us (7%)
    pallas_call x1, Pallas kernels, shards(): pl.pallas_call(functools.partial(attend, n), out_shape=jax.ShapeDtypeStru...  27.8 us
    unnamed x1, local copies, waits for them, and re-layouts  2.02 us

profile of v5, /device:TPU:1, one launch (start us, length us, event | category | flops | bytes accessed | tf_op | source)
XLA Modules:
  0.0 29.8 jit_solution(3327487444657057850)
XLA Ops:
  0.0 27.8 %shard_map.91 = bf16[2048,128]{1,0:T(8,128)(2,1)} custom-call(bf16[2048,128]{1,0:T(8,128)(2,1)} %bitcast.9, bf16[512,128]{1,0:T(8,128)(2,1)} %bitcast.10, bf16[512,128]{1,0:T(8,128)(2,1)} %bitcast.11, bf16[16,512,128]{2,1,0:T(8,128)(2,1)} %bitcast.6, bf16[16,512,128]{2,1,0:T(8,128)(2,1)} %bitcast.7, s32[2]{0:T(128)} %vp_ref.1, s32[1,6]{1,0:T(1,128)} %vl_ref.1, ...), custom_call_target="tpu_custom_call" | custom-call | tf_op jit(solution)/shard_map/pallas_call | solution.py:294
  27.8 2.0 %copy.11 = bf16[128,4,4,128]{3,2,1,0:T(4,128)(2,1)} copy(bf16[128,4,4,128]{3,2,1,0:T(4,128)(2,1)} %bitcast.8) | data formatting | bytes 1048576
